TPU v7x, 512 devices: a whole 4x4x16 slice. The times are simulated.
512 devices in a mesh: dp: 8 (over y, core), station: 64 (over x, z).
Axes of the slice: x: 4, y: 4, z: 16, core: 2. Of those that a mesh axis runs over, the one named last changes fastest.
Arguments:
- query_states: bfloat16 [8, 64, 128, 768], P('dp', 'station'), may hold values from -6 to 6
- key_states: bfloat16 [8, 64, 128, 768], P('dp', 'station'), may hold values from -6 to 6
- value_states: bfloat16 [8, 64, 128, 768], P('dp', 'station'), may hold values from -15 to 15
- grad_output: bfloat16 [8, 64, 128, 768], P('dp', 'station'), may hold values from -6 to 6
- out_weight: bfloat16 [768, 768], replicated, may hold values from -0.21875 to 0.21875
- partner_ids: int32 [64, 6], replicated, may hold values from 0 to 63, as said below
- partner_count: int32 [64], replicated, may hold values from 1 to 6, as said below
Outputs:
- layer_output: bfloat16 [8, 64, 128, 768], P('dp', 'station')
- grad_query: bfloat16 [8, 64, 128, 768], P('dp', 'station')
- grad_key: bfloat16 [8, 64, 128, 768], P('dp', 'station')
- grad_value: bfloat16 [8, 64, 128, 768], P('dp', 'station')
- grad_weight: float32 [768, 768], P('dp')
Inputs may be any that keep to these rules, and one draw needn't show every extreme that they name: `partner_ids`: row s lists 6 different stations other than s, all held by devices within 3 places of the device of s along the station axis, taken as a loop (station s lies on device s); only the first partner_count[s] entries are partners. `partner_count`: some station has exactly 6 partners.
All inputs are finite; a program needn't handle non-finite values.
Results may differ from a plain program's by a relative error of at most 0.025.
Values may be sent and summed in bfloat16 or wider, within the bound.
A program may use at most 64 MiB of HBM per device.

v0:
```python
import math
import jax
import jax.numpy as jnp
from jax import lax
from jax.sharding import PartitionSpec as P

HEADS = 12
PMAX = 6
HOPS = 3
neg_big = -1e30


def from_behind(value, axis, steps):
    count = lax.axis_size(axis)
    pairs = [(source, (source + steps) % count) for source in range(count)]
    return lax.ppermute(value, axis, pairs)


def split_heads(rows_in, head_count):
    return rows_in.reshape(rows_in.shape[:-1] + (head_count, rows_in.shape[-1] // head_count))


def local(
    query_states, key_states, value_states, grad_output, out_weight, partner_ids, partner_count
):
    window_count, per_device, span_rows, model_width = query_states.shape
    head_count = HEADS
    head_width = model_width // head_count
    score_scale = 1.0 / math.sqrt(head_width)
    slot_count = PMAX + 1
    device_count = lax.axis_size("station")
    station_count = per_device * device_count
    device_no = lax.axis_index("station")
    candidates = (2 * HOPS + 1) * per_device
    first_station = (device_no - HOPS) * per_device
    key_value = jnp.stack([key_states, value_states], 0)
    pieces = []
    for offset in range(-HOPS, HOPS + 1):
        if offset == 0:
            pieces.append(key_value)
        else:
            pieces.append(from_behind(key_value, "station", -offset))
    window = jnp.concatenate(pieces, 2)
    my_partners = lax.dynamic_slice_in_dim(partner_ids, device_no * per_device, per_device, 0)
    my_counts = lax.dynamic_slice_in_dim(partner_count, device_no * per_device, per_device, 0)
    partner_pos = jnp.mod(my_partners - first_station, station_count)
    self_pos = HOPS * per_device + jnp.arange(per_device, dtype=jnp.int32)
    slot_station = jnp.concatenate([self_pos[:, None], partner_pos], 1)
    slot_live = jnp.arange(slot_count, dtype=jnp.int32)[None, :] <= my_counts[:, None]
    row_count = window_count * per_device * span_rows
    flat_grad = grad_output.reshape(row_count, model_width)
    grad_mixed = lax.dot_general(
        flat_grad, out_weight, (((1,), (1,)), ((), ())), preferred_element_type=jnp.float32
    ).astype(jnp.bfloat16)
    grad_mixed = grad_mixed.reshape(query_states.shape)

    def one_station(number):
        window_no = number // per_device
        station_no = number % per_device
        query_rows = split_heads(query_states[window_no, station_no], head_count)
        grad_rows = split_heads(grad_mixed[window_no, station_no], head_count)
        picked = jnp.take(window[:, window_no], slot_station[station_no], axis=1)
        key_rows = picked[0].reshape(slot_count * span_rows, head_count, head_width)
        value_rows = picked[1].reshape(slot_count * span_rows, head_count, head_width)
        allowed = jnp.repeat(slot_live[station_no].astype(jnp.float32), span_rows)
        scores = (
            jnp.einsum("qhd,khd->hqk", query_rows, key_rows, preferred_element_type=jnp.float32)
            * score_scale
        )
        masked = jnp.where(allowed[None, None, :] > 0, scores, neg_big)
        row_max = jnp.max(masked, -1)
        weights_raw = jnp.exp(masked - row_max[..., None])
        row_sum = jnp.sum(weights_raw, -1)
        attn_probs = weights_raw / row_sum[..., None]
        probs_half = attn_probs.astype(jnp.bfloat16)
        mixed_rows = jnp.einsum(
            "hqk,khd->qhd", probs_half, value_rows, preferred_element_type=jnp.float32
        ).astype(jnp.bfloat16)
        row_delta = jnp.sum(grad_rows.astype(jnp.float32) * mixed_rows.astype(jnp.float32), -1).T
        grad_probs = jnp.einsum(
            "qhd,khd->hqk", grad_rows, value_rows, preferred_element_type=jnp.float32
        )
        grad_scores = (attn_probs * (grad_probs - row_delta[..., None])).astype(jnp.bfloat16)
        query_grad = (
            score_scale
            * jnp.einsum("hqk,khd->qhd", grad_scores, key_rows, preferred_element_type=jnp.float32)
        ).astype(jnp.bfloat16)
        result = (
            mixed_rows.reshape(span_rows, model_width),
            query_grad.reshape(span_rows, model_width),
        )
        key_part = score_scale * jnp.einsum(
            "hqk,qhd->khd", grad_scores, query_rows, preferred_element_type=jnp.float32
        )
        value_part = jnp.einsum(
            "hqk,qhd->khd", probs_half, grad_rows, preferred_element_type=jnp.float32
        )
        result = result + (
            jnp.stack([key_part, value_part], 0).reshape(2, -1, span_rows, model_width),
        )
        return result

    outputs = lax.map(one_station, jnp.arange(window_count * per_device, dtype=jnp.int32))
    mixed_all = outputs[0].reshape(query_states.shape)
    grad_query = outputs[1].reshape(query_states.shape)
    contribution = outputs[2].reshape(window_count, per_device, 2, -1, span_rows, model_width)
    moved = jnp.moveaxis(contribution, 2, 0).reshape(
        2, window_count, per_device * slot_count, span_rows, model_width
    )
    flat_slots = slot_station.reshape(-1)
    spread = (
        jnp.zeros((2, window_count, candidates, span_rows, model_width), jnp.float32)
        .at[:, :, flat_slots]
        .add(moved)
    )
    own_grads = spread[:, :, HOPS * per_device : (HOPS + 1) * per_device]
    for offset in range(-HOPS, HOPS + 1):
        if offset != 0:
            lower = (offset + HOPS) * per_device
            own_grads = own_grads + from_behind(
                spread[:, :, lower : lower + per_device].astype(jnp.bfloat16), "station", offset
            ).astype(jnp.float32)
    mixed_flat = mixed_all.reshape(row_count, model_width)
    layer_output = jnp.dot(mixed_flat, out_weight, preferred_element_type=jnp.float32).astype(
        jnp.bfloat16
    )
    grad_weight = lax.psum_scatter(
        lax.dot_general(
            mixed_flat, flat_grad, (((0,), (0,)), ((), ())), preferred_element_type=jnp.float32
        ).astype(jnp.bfloat16),
        "dp",
        scatter_dimension=0,
        tiled=True,
    ).astype(jnp.float32)
    grad_weight = lax.psum(grad_weight, "station")
    grad_weight = grad_weight / math.sqrt(row_count * lax.axis_size("dp") * device_count)
    return (
        layer_output.reshape(query_states.shape),
        grad_query,
        own_grads[0].astype(jnp.bfloat16),
        own_grads[1].astype(jnp.bfloat16),
        grad_weight,
    )


def solution(mesh):
    return jax.shard_map(
        local,
        mesh=mesh,
        in_specs=(
            P("dp", "station", None, None),
            P("dp", "station", None, None),
            P("dp", "station", None, None),
            P("dp", "station", None, None),
            P(),
            P(),
            P(),
        ),
        out_specs=(
            P("dp", "station", None, None),
            P("dp", "station", None, None),
            P("dp", "station", None, None),
            P("dp", "station", None, None),
            P("dp", None),
        ),
        check_vma=False,
    )
```

profile of v0, /device:TPU:24, one launch (start us, length us, event | category | flops | bytes accessed | tf_op | source)
XLA Modules:
  0.0 522.1 jit_solution(13839279402721123467)
XLA Ops:
  7.3 1.2 pad_maximum_fusion
  8.4 6.5 %collective-permute-start = (bf16[2,1,1,128,768]{4,3,2,1,0:T(8,128)(2,1)S(1)}, bf16[2,1,1,128,768]{4,3,2,1,0:T(8,128)(2,1)}, u32[]{:S(2)}, u32[]{:S(2)}) collective-permute-start(bf16[2,1,1,128,768]{4,3,2,1,0:T(8,128)(2,1)S(1)} %pad_maximum_fusion), channel_id=1, source_target_pairs={{0,3},{1,4},{2,5},{3,6},{4,7},{5,8},{6,9},{7,10},{8,11},{9,12},{10... | collective-permute-start | bytes 1179656 | tf_op jit(solution)/shard_map/ppermute | solution.py:16
  15.0 6.4 %collective-permute-start.1 = (bf16[2,1,1,128,768]{4,3,2,1,0:T(8,128)(2,1)S(1)}, bf16[2,1,1,128,768]{4,3,2,1,0:T(8,128)(2,1)}, u32[]{:S(2)}, u32[]{:S(2)}) collective-permute-start(bf16[2,1,1,128,768]{4,3,2,1,0:T(8,128)(2,1)S(1)} %pad_maximum_fusion), channel_id=1, source_target_pairs={{0,2},{1,3},{2,4},{3,5},{4,6},{5,7},{6,8},{7,9},{8,10},{9,11},{10,... | collective-permute-start | bytes 1179656 | tf_op jit(solution)/shard_map/ppermute | solution.py:16
  21.4 3.8 collective-permute-start.2
  25.2 5.3 %collective-permute-start.3 = (bf16[2,1,1,128,768]{4,3,2,1,0:T(8,128)(2,1)S(1)}, bf16[2,1,1,128,768]{4,3,2,1,0:T(8,128)(2,1)S(1)}, u32[]{:S(2)}, u32[]{:S(2)}) collective-permute-start(bf16[2,1,1,128,768]{4,3,2,1,0:T(8,128)(2,1)S(1)} %pad_maximum_fusion), channel_id=1, source_target_pairs={{0,63},{1,0},{2,1},{3,2},{4,3},{5,4},{6,5},{7,6},{8,7},{9,8},{10,9... | collective-permute-start | bytes 1179656 | tf_op jit(solution)/shard_map/ppermute | solution.py:16
  30.6 2.1 collective-permute-start.4
  32.7 1.2 dynamic_slice.20
  33.9 0.7 fusion.22
  34.6 1.5 convolution_convert_fusion.2
  36.1 0.8 add_select_fusion
  36.9 0.1 add_reduce_fusion
  37.0 0.2 copy.39
  37.2 0.2 copy.37
  37.4 11.0 %collective-permute-done = bf16[2,1,1,128,768]{4,3,2,1,0:T(8,128)(2,1)} collective-permute-done((bf16[2,1,1,128,768]{4,3,2,1,0:T(8,128)(2,1)S(1)}, bf16[2,1,1,128,768]{4,3,2,1,0:T(8,128)(2,1)}, u32[]{:S(2)}, u32[]{:S(2)}) %collective-permute-start) | collective-permute-done | bytes 393248 | tf_op jit(solution)/shard_map/ppermute | solution.py:16
  48.4 5.5 %collective-permute-start.5 = (bf16[2,1,1,128,768]{4,3,2,1,0:T(8,128)(2,1)S(1)}, bf16[2,1,1,128,768]{4,3,2,1,0:T(8,128)(2,1)S(1)}, u32[]{:S(2)}, u32[]{:S(2)}) collective-permute-start(bf16[2,1,1,128,768]{4,3,2,1,0:T(8,128)(2,1)S(1)} %pad_maximum_fusion), channel_id=1, source_target_pairs={{0,61},{1,62},{2,63},{3,0},{4,1},{5,2},{6,3},{7,4},{8,5},{9,6},{10... | collective-permute-start | bytes 1179656 | tf_op jit(solution)/shard_map/ppermute | solution.py:16
  53.9 1.8 constant_dynamic-update-slice_fusion.6
  55.7 8.0 %collective-permute-done.1 = bf16[2,1,1,128,768]{4,3,2,1,0:T(8,128)(2,1)} collective-permute-done((bf16[2,1,1,128,768]{4,3,2,1,0:T(8,128)(2,1)S(1)}, bf16[2,1,1,128,768]{4,3,2,1,0:T(8,128)(2,1)}, u32[]{:S(2)}, u32[]{:S(2)}) %collective-permute-start.1) | collective-permute-done | bytes 393248 | tf_op jit(solution)/shard_map/ppermute | solution.py:16
  63.7 1.8 constant_dynamic-update-slice_fusion.5
  65.5 8.0 %collective-permute-done.2 = bf16[2,1,1,128,768]{4,3,2,1,0:T(8,128)(2,1)} collective-permute-done((bf16[2,1,1,128,768]{4,3,2,1,0:T(8,128)(2,1)S(1)}, bf16[2,1,1,128,768]{4,3,2,1,0:T(8,128)(2,1)}, u32[]{:S(2)}, u32[]{:S(2)}) %collective-permute-start.2) | collective-permute-done | bytes 393248 | tf_op jit(solution)/shard_map/ppermute | solution.py:16
  73.5 1.8 constant_dynamic-update-slice_fusion.4
  75.3 0.8 constant_dynamic-update-slice_fusion.3
  76.1 0.8 constant_dynamic-update-slice_fusion.2
  76.8 0.8 constant_dynamic-update-slice_fusion.1
  77.6 0.9 collective-permute-done.5
  78.5 0.8 constant_dynamic-update-slice_fusion
  79.3 4.1 gather_fusion
  83.4 2.1 select_bitcast_fusion
  85.6 1.7 fusion.27
  87.3 2.1 copy.35
  89.4 2.5 squeeze.36
  91.9 2.1 copy.36
  94.0 2.5 squeeze.37
  96.5 5.9 %fusion.28 = (f32[12,128]{1,0:T(8,128)S(1)}, f32[12,128,896]{1,2,0:T(8,128)}) fusion(pred[896]{0:T(1024)(128)(4,1)S(1)} %broadcast_bitcast_fusion, bf16[896,12,64]{0,2,1:T(8,128)(2,1)} %squeeze.37, bf16[128,12,64]{0,2,1:T(8,128)(2,1)S(1)} %bitcast.88), kind=kOutput, calls=%fused_computation.65 | convolution fusion | flops 181666688 | bytes 7084928 | tf_op jit(solution)/shard_map/while/body/eval_jaxpr/sub | solution.py:72
  102.4 3.3 fusion.8
  105.7 2.7 convolution_bitcast_fusion
  108.4 0.7 multiply_reduce_fusion
  109.1 2.9 multiply_convert_fusion
  112.0 4.2 stack.25
  116.2 4.5 multiply_bitcast_fusion
  120.7 4.2 stack.24
  124.9 1.5 convolution_convert_fusion
  126.4 6.1 %maximum_bitcast_fusion = f32[7,2,128,768]{2,0,3,1:T(8,128)} fusion(f32[1,1,7,128,768]{3,2,4,1,0:T(8,128)} %stack.25, f32[1,1,7,128,768]{3,2,4,1,0:T(8,128)} %stack.24), kind=kLoop, calls=%fused_computation.3 | loop fusion | flops 1376256 | bytes 11010048 | tf_op jit(solution)/shard_map/while/body/eval_jaxpr/stack | solution.py:99
  132.5 6.4 %copy.44 = f32[7,2,128,768]{3,2,1,0:T(8,128)} copy(f32[7,2,128,768]{2,0,3,1:T(8,128)} %maximum_bitcast_fusion) | data formatting | bytes 11010048 | tf_op jit(solution)/shard_map/while/body/eval_jaxpr/stack | solution.py:99
  138.9 3.0 broadcast.96
  141.8 14.2 %scatter_fusion = f32[2,7,128,768]{3,2,1,0:T(8,128)} fusion(f32[2,7,128,768]{3,2,1,0:T(8,128)} %broadcast.96, s32[7]{0:T(128)S(1)} %fusion.23, f32[7,2,128,768]{3,2,1,0:T(8,128)} %copy.44), kind=kCustom, calls=%fused_computation.1 | custom fusion | flops 1376256 | bytes 16515100 | tf_op jit(solution)/shard_map/scatter-add | solution.py:114
  156.0 2.9 bitcast_convert_fusion
  158.9 1.1 fusion.26
  160.0 2.7 collective-permute-start.11
  162.7 10.5 %collective-permute-start.10 = (bf16[2,1,1,128,768]{4,3,2,0,1:T(8,128)(2,1)}, bf16[2,1,1,128,768]{4,3,2,0,1:T(8,128)(2,1)S(1)}, u32[]{:S(2)}, u32[]{:S(2)}) collective-permute-start(bf16[2,1,1,128,768]{4,3,2,0,1:T(8,128)(2,1)} %get-tuple-element.49), channel_id=1, source_target_pairs={{0,2},{1,3},{2,4},{3,5},{4,6},{5,7},{6,8},{7,9},{8,10},{9,11},{10,... | collective-permute-start | bytes 1179656 | tf_op jit(solution)/shard_map/ppermute | solution.py:16
  173.2 2.4 collective-permute-start.9
  175.6 6.7 %collective-permute-start.8 = (bf16[2,1,1,128,768]{4,3,2,0,1:T(8,128)(2,1)}, bf16[2,1,1,128,768]{4,3,2,0,1:T(8,128)(2,1)}, u32[]{:S(2)}, u32[]{:S(2)}) collective-permute-start(bf16[2,1,1,128,768]{4,3,2,0,1:T(8,128)(2,1)} %get-tuple-element.51), channel_id=1, source_target_pairs={{0,63},{1,0},{2,1},{3,2},{4,3},{5,4},{6,5},{7,6},{8,7},{9,8},{10,9... | collective-permute-start | bytes 1179656 | tf_op jit(solution)/shard_map/ppermute | solution.py:16
  182.3 2.1 collective-permute-start.7
  184.5 11.3 %collective-permute-done.11 = bf16[2,1,1,128,768]{4,3,2,0,1:T(8,128)(2,1)S(1)} collective-permute-done((bf16[2,1,1,128,768]{4,3,2,0,1:T(8,128)(2,1)S(1)}, bf16[2,1,1,128,768]{4,3,2,0,1:T(8,128)(2,1)S(1)}, u32[]{:S(2)}, u32[]{:S(2)}) %collective-permute-start.11) | collective-permute-done | bytes 393248 | tf_op jit(solution)/shard_map/ppermute | solution.py:16
  195.7 1.9 collective-permute-start.6
  197.6 0.7 fusion.9
  198.3 0.8 copy.45
  199.2 1.0 fusion.10
  200.2 9.9 %collective-permute-done.10 = bf16[2,1,1,128,768]{4,3,2,0,1:T(8,128)(2,1)S(1)} collective-permute-done((bf16[2,1,1,128,768]{4,3,2,0,1:T(8,128)(2,1)}, bf16[2,1,1,128,768]{4,3,2,0,1:T(8,128)(2,1)S(1)}, u32[]{:S(2)}, u32[]{:S(2)}) %collective-permute-start.10) | collective-permute-done | bytes 393248 | tf_op jit(solution)/shard_map/ppermute | solution.py:16
  210.1 9.8 %collective-permute-done.9 = bf16[2,1,1,128,768]{4,3,2,0,1:T(8,128)(2,1)S(1)} collective-permute-done((bf16[2,1,1,128,768]{4,3,2,0,1:T(8,128)(2,1)}, bf16[2,1,1,128,768]{4,3,2,0,1:T(8,128)(2,1)S(1)}, u32[]{:S(2)}, u32[]{:S(2)}) %collective-permute-start.9) | collective-permute-done | bytes 393248 | tf_op jit(solution)/shard_map/ppermute | solution.py:16
  220.0 8.0 %collective-permute-done.6 = bf16[2,1,1,128,768]{4,3,2,0,1:T(8,128)(2,1)} collective-permute-done((bf16[2,1,1,128,768]{4,3,2,0,1:T(8,128)(2,1)S(1)}, bf16[2,1,1,128,768]{4,3,2,0,1:T(8,128)(2,1)}, u32[]{:S(2)}, u32[]{:S(2)}) %collective-permute-start.6) | collective-permute-done | bytes 393248 | tf_op jit(solution)/shard_map/ppermute | solution.py:16
  227.9 1.8 fusion.16
  229.7 0.8 slice_bitcast_fusion
  230.5 284.0 %all-reduce.1 = f32[96,768]{1,0:T(8,128)S(1)} all-reduce(bf16[96,768]{1,0:T(8,128)(2,1)} %reduce-scatter.2.cloned.1.call-done), channel_id=1, replica_groups=mesh['dp'=8,'station'=64] {'station'}, use_global_device_ids=true, to_apply=%region_5.6 | all-reduce | flops 73728 | bytes 442368 | tf_op jit(solution)/shard_map/psum | solution.py:135
  514.5 0.7 broadcast_multiply_fusion
  (32 shorter events, 0.2 us)
Async XLA Ops:
  7.2 27.5 %copy-start = (bf16[768,768]{1,0:T(8,128)(2,1)S(1)}, bf16[768,768]{1,0:T(8,128)(2,1)}, u32[]{:S(2)}) copy-start(bf16[768,768]{1,0:T(8,128)(2,1)} %param.11) | copy-start | bytes 3538948
  7.2 30.0 %copy-start.7 = (bf16[1,1,128,768]{3,2,1,0:T(8,128)(2,1)S(1)}, bf16[1,1,128,768]{3,2,1,0:T(8,128)(2,1)}, u32[]{:S(2)}) copy-start(bf16[1,1,128,768]{3,2,1,0:T(8,128)(2,1)} %param.7) | copy-start | bytes 589828
  7.2 223.3 %reduce-scatter.2.cloned.1.call-start = ((), (), s32[]{:S(2)}) async-start(), calls=%async_computation.1 | async-start | bytes 1327104 | tf_op jit(solution)/shard_map/reduce_scatter | solution.py:127
  7.2 68.0 %copy-start.5 = (bf16[1,1,128,768]{3,2,1,0:T(8,128)(2,1)S(1)}, bf16[1,1,128,768]{3,2,1,0:T(8,128)(2,1)}, u32[]{:S(2)}) copy-start(bf16[1,1,128,768]{3,2,1,0:T(8,128)(2,1)} %param.9) | copy-start | bytes 589828
  7.2 68.0 %copy-start.6 = (bf16[1,1,128,768]{3,2,1,0:T(8,128)(2,1)S(1)}, bf16[1,1,128,768]{3,2,1,0:T(8,128)(2,1)}, u32[]{:S(2)}) copy-start(bf16[1,1,128,768]{3,2,1,0:T(8,128)(2,1)} %param.8) | copy-start | bytes 589828
  8.4 40.0 %collective-permute-start = (bf16[2,1,1,128,768]{4,3,2,1,0:T(8,128)(2,1)S(1)}, bf16[2,1,1,128,768]{4,3,2,1,0:T(8,128)(2,1)}, u32[]{:S(2)}, u32[]{:S(2)}) collective-permute-start(bf16[2,1,1,128,768]{4,3,2,1,0:T(8,128)(2,1)S(1)} %pad_maximum_fusion), channel_id=1, source_target_pairs={{0,3},{1,4},{2,5},{3,6},{4,7},{5,8},{6,9},{7,10},{8,11},{9,12},{10... | collective-permute-start | bytes 1179656 | tf_op jit(solution)/shard_map/ppermute | solution.py:16
  15.0 48.7 %collective-permute-start.1 = (bf16[2,1,1,128,768]{4,3,2,1,0:T(8,128)(2,1)S(1)}, bf16[2,1,1,128,768]{4,3,2,1,0:T(8,128)(2,1)}, u32[]{:S(2)}, u32[]{:S(2)}) collective-permute-start(bf16[2,1,1,128,768]{4,3,2,1,0:T(8,128)(2,1)S(1)} %pad_maximum_fusion), channel_id=1, source_target_pairs={{0,2},{1,3},{2,4},{3,5},{4,6},{5,7},{6,8},{7,9},{8,10},{9,11},{10,... | collective-permute-start | bytes 1179656 | tf_op jit(solution)/shard_map/ppermute | solution.py:16
  21.4 52.1 %collective-permute-start.2 = (bf16[2,1,1,128,768]{4,3,2,1,0:T(8,128)(2,1)S(1)}, bf16[2,1,1,128,768]{4,3,2,1,0:T(8,128)(2,1)}, u32[]{:S(2)}, u32[]{:S(2)}) collective-permute-start(bf16[2,1,1,128,768]{4,3,2,1,0:T(8,128)(2,1)S(1)} %pad_maximum_fusion), channel_id=1, source_target_pairs={{0,1},{1,2},{2,3},{3,4},{4,5},{5,6},{6,7},{7,8},{8,9},{9,10},{10,1... | collective-permute-start | bytes 1179656 | tf_op jit(solution)/shard_map/ppermute | solution.py:16
  25.2 50.8 %collective-permute-start.3 = (bf16[2,1,1,128,768]{4,3,2,1,0:T(8,128)(2,1)S(1)}, bf16[2,1,1,128,768]{4,3,2,1,0:T(8,128)(2,1)S(1)}, u32[]{:S(2)}, u32[]{:S(2)}) collective-permute-start(bf16[2,1,1,128,768]{4,3,2,1,0:T(8,128)(2,1)S(1)} %pad_maximum_fusion), channel_id=1, source_target_pairs={{0,63},{1,0},{2,1},{3,2},{4,3},{5,4},{6,5},{7,6},{8,7},{9,8},{10,9... | collective-permute-start | bytes 1179656 | tf_op jit(solution)/shard_map/ppermute | solution.py:16
  30.6 46.3 %collective-permute-start.4 = (bf16[2,1,1,128,768]{4,3,2,1,0:T(8,128)(2,1)S(1)}, bf16[2,1,1,128,768]{4,3,2,1,0:T(8,128)(2,1)S(1)}, u32[]{:S(2)}, u32[]{:S(2)}) collective-permute-start(bf16[2,1,1,128,768]{4,3,2,1,0:T(8,128)(2,1)S(1)} %pad_maximum_fusion), channel_id=1, source_target_pairs={{0,62},{1,63},{2,0},{3,1},{4,2},{5,3},{6,4},{7,5},{8,6},{9,7},{10,... | collective-permute-start | bytes 1179656 | tf_op jit(solution)/shard_map/ppermute | solution.py:16
  48.4 30.1 %collective-permute-start.5 = (bf16[2,1,1,128,768]{4,3,2,1,0:T(8,128)(2,1)S(1)}, bf16[2,1,1,128,768]{4,3,2,1,0:T(8,128)(2,1)S(1)}, u32[]{:S(2)}, u32[]{:S(2)}) collective-permute-start(bf16[2,1,1,128,768]{4,3,2,1,0:T(8,128)(2,1)S(1)} %pad_maximum_fusion), channel_id=1, source_target_pairs={{0,61},{1,62},{2,63},{3,0},{4,1},{5,2},{6,3},{7,4},{8,5},{9,6},{10... | collective-permute-start | bytes 1179656 | tf_op jit(solution)/shard_map/ppermute | solution.py:16
  102.4 6.7 %slice-start = ((s8[5505024]{0:T(1024)(128)(4,1)}), s8[4194304]{0:T(1024)(128)(4,1)S(1)}, s32[]{:S(2)}) async-start(s8[5505024]{0:T(1024)(128)(4,1)} %bitcast.81), calls=%async_computation.2 | async-start | bytes 8388608
  105.7 2.7 copy-start.3
  105.7 3.4 slice-start.1
  120.7 4.2 copy-start.4
  158.9 38.7 %copy-start.1 = (bf16[12,128,896]{1,2,0:T(8,128)(2,1)S(1)}, bf16[12,128,896]{1,2,0:T(8,128)(2,1)}, u32[]{:S(2)}) copy-start(bf16[12,128,896]{1,2,0:T(8,128)(2,1)} %multiply_convert_fusion) | copy-start | bytes 8257540
  158.9 38.7 %copy-start.2 = (bf16[896,12,64]{0,2,1:T(8,128)(2,1)S(1)}, bf16[896,12,64]{0,2,1:T(8,128)(2,1)}, u32[]{:S(2)}) copy-start(bf16[896,12,64]{0,2,1:T(8,128)(2,1)} %squeeze.37) | copy-start | bytes 4128772
  160.0 35.7 %collective-permute-start.11 = (bf16[2,1,1,128,768]{4,3,2,0,1:T(8,128)(2,1)S(1)}, bf16[2,1,1,128,768]{4,3,2,0,1:T(8,128)(2,1)S(1)}, u32[]{:S(2)}, u32[]{:S(2)}) collective-permute-start(bf16[2,1,1,128,768]{4,3,2,0,1:T(8,128)(2,1)S(1)} %get-tuple-element.48), channel_id=1, source_target_pairs={{0,3},{1,4},{2,5},{3,6},{4,7},{5,8},{6,9},{7,10},{8,11},{9,12},{10... | collective-permute-start | bytes 1179656 | tf_op jit(solution)/shard_map/ppermute | solution.py:16
  162.7 47.4 %collective-permute-start.10 = (bf16[2,1,1,128,768]{4,3,2,0,1:T(8,128)(2,1)}, bf16[2,1,1,128,768]{4,3,2,0,1:T(8,128)(2,1)S(1)}, u32[]{:S(2)}, u32[]{:S(2)}) collective-permute-start(bf16[2,1,1,128,768]{4,3,2,0,1:T(8,128)(2,1)} %get-tuple-element.49), channel_id=1, source_target_pairs={{0,2},{1,3},{2,4},{3,5},{4,6},{5,7},{6,8},{7,9},{8,10},{9,11},{10,... | collective-permute-start | bytes 1179656 | tf_op jit(solution)/shard_map/ppermute | solution.py:16
  173.2 46.8 %collective-permute-start.9 = (bf16[2,1,1,128,768]{4,3,2,0,1:T(8,128)(2,1)}, bf16[2,1,1,128,768]{4,3,2,0,1:T(8,128)(2,1)S(1)}, u32[]{:S(2)}, u32[]{:S(2)}) collective-permute-start(bf16[2,1,1,128,768]{4,3,2,0,1:T(8,128)(2,1)} %get-tuple-element.50), channel_id=1, source_target_pairs={{0,1},{1,2},{2,3},{3,4},{4,5},{5,6},{6,7},{7,8},{8,9},{9,10},{10,1... | collective-permute-start | bytes 1179656 | tf_op jit(solution)/shard_map/ppermute | solution.py:16
  175.6 44.4 %collective-permute-start.8 = (bf16[2,1,1,128,768]{4,3,2,0,1:T(8,128)(2,1)}, bf16[2,1,1,128,768]{4,3,2,0,1:T(8,128)(2,1)}, u32[]{:S(2)}, u32[]{:S(2)}) collective-permute-start(bf16[2,1,1,128,768]{4,3,2,0,1:T(8,128)(2,1)} %get-tuple-element.51), channel_id=1, source_target_pairs={{0,63},{1,0},{2,1},{3,2},{4,3},{5,4},{6,5},{7,6},{8,7},{9,8},{10,9... | collective-permute-start | bytes 1179656 | tf_op jit(solution)/shard_map/ppermute | solution.py:16
  182.3 37.6 %collective-permute-start.7 = (bf16[2,1,1,128,768]{4,3,2,0,1:T(8,128)(2,1)S(1)}, bf16[2,1,1,128,768]{4,3,2,0,1:T(8,128)(2,1)}, u32[]{:S(2)}, u32[]{:S(2)}) collective-permute-start(bf16[2,1,1,128,768]{4,3,2,0,1:T(8,128)(2,1)S(1)} %get-tuple-element.52), channel_id=1, source_target_pairs={{0,62},{1,63},{2,0},{3,1},{4,2},{5,3},{6,4},{7,5},{8,6},{9,7},{10,... | collective-permute-start | bytes 1179656 | tf_op jit(solution)/shard_map/ppermute | solution.py:16
  195.7 32.2 %collective-permute-start.6 = (bf16[2,1,1,128,768]{4,3,2,0,1:T(8,128)(2,1)S(1)}, bf16[2,1,1,128,768]{4,3,2,0,1:T(8,128)(2,1)}, u32[]{:S(2)}, u32[]{:S(2)}) collective-permute-start(bf16[2,1,1,128,768]{4,3,2,0,1:T(8,128)(2,1)S(1)} %get-tuple-element.47), channel_id=1, source_target_pairs={{0,61},{1,62},{2,63},{3,0},{4,1},{5,2},{6,3},{7,4},{8,5},{9,6},{10... | collective-permute-start | bytes 1179656 | tf_op jit(solution)/shard_map/ppermute | solution.py:16
Sparse Core Ops, SparseCore 0:
  126.5 36.0 reduce-scatter.1
where the time goes:
time: 523 us; the launch traced here: 522 us
  blocking collectives  284 us (54%)
  waiting for transfers between devices  67.1 us (13%)
  starting transfers between devices  56.1 us (11%)
  local copies, waits for them, and re-layouts  44.7 us (9%)
  other arithmetic  34.6 us (7%)
  matrix products  21.4 us (4%)
  between operations  14.3 us (3%)
    psum x1, blocking collectives, local(): grad_weight = lax.psum(grad_weight, 'station')  284 us
    ppermute x12, waiting for transfers between devices, from_behind(): return lax.ppermute(value, axis, pairs)  67 us
    ppermute x12, starting transfers between devices, from_behind(): return lax.ppermute(value, axis, pairs)  56 us
    another operation x3, local copies, waits for them, and re-layouts, one_station(): jnp.stack([key_part, value_part], 0).reshape(2, -1, span_rows, model_width)  14.7 us
    scatter-add x1, other arithmetic, local(): spread = jnp.zeros((2, window_count, candidates, span_rows, model_width),...  14.2 us
  transfers between devices with their start and end apart: 13, of which 8 were waited for; matrix products, arithmetic and copies ran while one was open for 10% of the time, Pallas kernels for 0%

commit v1 on v0

--- a/solution.py
+++ b/solution.py
@@ -132,7 +132,7 @@
         scatter_dimension=0,
         tiled=True,
     ).astype(jnp.float32)
-    grad_weight = lax.psum(grad_weight, "station")
+    grad_weight = jnp.sum(lax.all_gather(grad_weight, "station"), axis=0)
     grad_weight = grad_weight / math.sqrt(row_count * lax.axis_size("dp") * device_count)
     return (
         layer_output.reshape(query_states.shape),

time: 523 us -> 392 us (0.75)
  blocking collectives: 284 us -> 0 us
  waiting for transfers between devices: 67.1 us -> 205 us
  other arithmetic: 34.6 us -> 43.6 us
    psum x1 -> x0, blocking collectives: 284 us -> none  [local(): grad_weight = lax.psum(grad_weight, 'station')]
    all_gather x0 -> x1, waiting for transfers between devices: none -> 86.3 us  [local(): grad_weight = jnp.sum(lax.all_gather(grad_weight, 'station'), axis=0)]
    reduce_scatter x1, waiting for transfers between devices: 0.01 us -> 36 us  [local(): lax.psum_scatter(lax.dot_general(mixed_flat, flat_grad, (((0,), (0,)), ((...]
    ppermute x12, waiting for transfers between devices: 67 us -> 82.9 us  [from_behind(): return lax.ppermute(value, axis, pairs)]
    reduce_sum x0 -> x1, other arithmetic: none -> 7.33 us  [local(): grad_weight = jnp.sum(lax.all_gather(grad_weight, 'station'), axis=0)]
  transfers between devices with their start and end apart: 13 -> 14, of which waited for: 8 -> 10; matrix products, arithmetic and copies ran while one was open for 10% -> 18% of each run, Pallas kernels for 0% -> 0%
where the time goes in v1:
time: 392 us; the launch traced here: 390 us
  waiting for transfers between devices  205 us (52%)
  starting transfers between devices  57.1 us (15%)
  local copies, waits for them, and re-layouts  47.7 us (12%)
  other arithmetic  43.6 us (11%)
  matrix products  22.4 us (6%)
  between operations  14.3 us (4%)
    all_gather x1, waiting for transfers between devices, local(): grad_weight = jnp.sum(lax.all_gather(grad_weight, 'station'), axis=0)  86.3 us
    ppermute x12, waiting for transfers between devices, from_behind(): return lax.ppermute(value, axis, pairs)  82.9 us
    ppermute x12, starting transfers between devices, from_behind(): return lax.ppermute(value, axis, pairs)  56.8 us
    reduce_scatter x1, waiting for transfers between devices, local(): lax.psum_scatter(lax.dot_general(mixed_flat, flat_grad, (((0,), (0,)), ((...  36 us
    another operation x3, local copies, waits for them, and re-layouts, one_station(): jnp.stack([key_part, value_part], 0).reshape(2, -1, span_rows, model_width)  14.6 us
    scatter-add x1, other arithmetic, local(): spread = jnp.zeros((2, window_count, candidates, span_rows, model_width),...  14.2 us
    unnamed x27, local copies, waits for them, and re-layouts  11 us
  transfers between devices with their start and end apart: 14, of which 10 were waited for; matrix products, arithmetic and copies ran while one was open for 18% of the time, Pallas kernels for 0%

profile of v1, /device:TPU:24, one launch (start us, length us, event | category | flops | bytes accessed | tf_op | source)
XLA Modules:
  0.0 390.4 jit_solution(12407170018343535910)
XLA Ops:
  7.3 1.2 pad_maximum_fusion
  8.4 6.5 %collective-permute-start = (bf16[2,1,1,128,768]{4,3,2,1,0:T(8,128)(2,1)S(1)}, bf16[2,1,1,128,768]{4,3,2,1,0:T(8,128)(2,1)}, u32[]{:S(2)}, u32[]{:S(2)}) collective-permute-start(bf16[2,1,1,128,768]{4,3,2,1,0:T(8,128)(2,1)S(1)} %pad_maximum_fusion), channel_id=1, source_target_pairs={{0,3},{1,4},{2,5},{3,6},{4,7},{5,8},{6,9},{7,10},{8,11},{9,12},{10... | collective-permute-start | bytes 1179656 | tf_op jit(solution)/shard_map/ppermute | solution.py:16
  15.0 6.4 %collective-permute-start.1 = (bf16[2,1,1,128,768]{4,3,2,1,0:T(8,128)(2,1)S(1)}, bf16[2,1,1,128,768]{4,3,2,1,0:T(8,128)(2,1)}, u32[]{:S(2)}, u32[]{:S(2)}) collective-permute-start(bf16[2,1,1,128,768]{4,3,2,1,0:T(8,128)(2,1)S(1)} %pad_maximum_fusion), channel_id=1, source_target_pairs={{0,2},{1,3},{2,4},{3,5},{4,6},{5,7},{6,8},{7,9},{8,10},{9,11},{10,... | collective-permute-start | bytes 1179656 | tf_op jit(solution)/shard_map/ppermute | solution.py:16
  21.4 3.8 collective-permute-start.2
  25.2 5.3 %collective-permute-start.3 = (bf16[2,1,1,128,768]{4,3,2,1,0:T(8,128)(2,1)S(1)}, bf16[2,1,1,128,768]{4,3,2,1,0:T(8,128)(2,1)S(1)}, u32[]{:S(2)}, u32[]{:S(2)}) collective-permute-start(bf16[2,1,1,128,768]{4,3,2,1,0:T(8,128)(2,1)S(1)} %pad_maximum_fusion), channel_id=1, source_target_pairs={{0,63},{1,0},{2,1},{3,2},{4,3},{5,4},{6,5},{7,6},{8,7},{9,8},{10,9... | collective-permute-start | bytes 1179656 | tf_op jit(solution)/shard_map/ppermute | solution.py:16
  30.6 2.1 collective-permute-start.4
  32.7 1.2 dynamic_slice.20
  34.6 1.5 convolution_convert_fusion.2
  36.1 0.8 add_select_fusion
  37.4 11.0 %collective-permute-done = bf16[2,1,1,128,768]{4,3,2,1,0:T(8,128)(2,1)} collective-permute-done((bf16[2,1,1,128,768]{4,3,2,1,0:T(8,128)(2,1)S(1)}, bf16[2,1,1,128,768]{4,3,2,1,0:T(8,128)(2,1)}, u32[]{:S(2)}, u32[]{:S(2)}) %collective-permute-start) | collective-permute-done | bytes 393248 | tf_op jit(solution)/shard_map/ppermute | solution.py:16
  48.4 5.5 %collective-permute-start.5 = (bf16[2,1,1,128,768]{4,3,2,1,0:T(8,128)(2,1)S(1)}, bf16[2,1,1,128,768]{4,3,2,1,0:T(8,128)(2,1)S(1)}, u32[]{:S(2)}, u32[]{:S(2)}) collective-permute-start(bf16[2,1,1,128,768]{4,3,2,1,0:T(8,128)(2,1)S(1)} %pad_maximum_fusion), channel_id=1, source_target_pairs={{0,61},{1,62},{2,63},{3,0},{4,1},{5,2},{6,3},{7,4},{8,5},{9,6},{10... | collective-permute-start | bytes 1179656 | tf_op jit(solution)/shard_map/ppermute | solution.py:16
  53.9 1.8 constant_dynamic-update-slice_fusion.6
  55.7 8.0 %collective-permute-done.1 = bf16[2,1,1,128,768]{4,3,2,1,0:T(8,128)(2,1)} collective-permute-done((bf16[2,1,1,128,768]{4,3,2,1,0:T(8,128)(2,1)S(1)}, bf16[2,1,1,128,768]{4,3,2,1,0:T(8,128)(2,1)}, u32[]{:S(2)}, u32[]{:S(2)}) %collective-permute-start.1) | collective-permute-done | bytes 393248 | tf_op jit(solution)/shard_map/ppermute | solution.py:16
  63.7 1.8 constant_dynamic-update-slice_fusion.5
  65.5 8.0 %collective-permute-done.2 = bf16[2,1,1,128,768]{4,3,2,1,0:T(8,128)(2,1)} collective-permute-done((bf16[2,1,1,128,768]{4,3,2,1,0:T(8,128)(2,1)S(1)}, bf16[2,1,1,128,768]{4,3,2,1,0:T(8,128)(2,1)}, u32[]{:S(2)}, u32[]{:S(2)}) %collective-permute-start.2) | collective-permute-done | bytes 393248 | tf_op jit(solution)/shard_map/ppermute | solution.py:16
  73.5 1.8 constant_dynamic-update-slice_fusion.4
  75.3 0.8 constant_dynamic-update-slice_fusion.3
  76.1 0.8 constant_dynamic-update-slice_fusion.2
  76.8 0.8 constant_dynamic-update-slice_fusion.1
  77.6 0.9 collective-permute-done.5
  78.5 0.8 constant_dynamic-update-slice_fusion
  79.3 4.1 %gather_fusion = bf16[7,2,128,768]{3,2,1,0:T(8,128)(2,1)} fusion(bf16[2,7,128,768]{3,2,1,0:T(8,128)(2,1)} %bitcast.2, s32[1024]{0:T(1024)S(1)} %pad_clamp_fusion), kind=kCustom, calls=%fused_computation | custom fusion | bytes 5505052 | tf_op jit(solution)/shard_map/while/body/eval_jaxpr/jit(_take)/gather | solution.py:62
  83.5 2.1 select_bitcast_fusion
  85.6 1.7 fusion.27
  87.3 2.1 copy.35
  89.4 2.5 squeeze.36
  91.8 2.1 copy.36
  94.0 2.5 squeeze.37
  96.5 5.9 %fusion.28 = (f32[12,128]{1,0:T(8,128)S(1)}, f32[12,128,896]{1,2,0:T(8,128)}) fusion(pred[896]{0:T(1024)(128)(4,1)S(1)} %broadcast_bitcast_fusion, bf16[896,12,64]{0,2,1:T(8,128)(2,1)} %squeeze.37, bf16[128,12,64]{0,2,1:T(8,128)(2,1)S(1)} %bitcast.88), kind=kOutput, calls=%fused_computation.65 | convolution fusion | flops 181666688 | bytes 7084928 | tf_op jit(solution)/shard_map/while/body/eval_jaxpr/sub | solution.py:72
  102.4 3.2 fusion.8
  105.6 1.6 copy-done.1
  107.2 0.7 multiply_reduce_fusion
  107.9 1.5 convolution_convert_fusion
  109.7 36.0 %reduce-scatter.2.cloned.1.call-done = bf16[96,768]{1,0:T(8,128)(2,1)} async-done(((bf16[768,768]{1,0:T(8,128)(2,1)}), bf16[96,768]{1,0:T(8,128)(2,1)}) %reduce-scatter.2.cloned.1.call-update) | async-done | bytes 147472 | tf_op jit(solution)/shard_map/reduce_scatter | solution.py:127
  145.7 1.6 all_gather.12
  147.4 4.6 %convolution_bitcast_fusion = f32[896,12,64]{0,2,1:T(8,128)} fusion(bf16[128,12,64]{0,2,1:T(8,128)(2,1)S(1)} %bitcast.84, bf16[12,128,896]{1,2,0:T(8,128)(2,1)} %copy-done.1), kind=kOutput, calls=%fused_computation.17 | convolution fusion | flops 176160768 | bytes 5701632 | tf_op jit(solution)/shard_map/while/body/eval_jaxpr/hqk,qhd->khd/dot_general | solution.py:95
  152.0 4.1 %stack.25 = f32[1,1,7,128,768]{3,2,4,1,0:T(8,128)} reshape(f32[896,12,64]{0,2,1:T(8,128)} %convolution_bitcast_fusion) | data formatting | bytes 5505024 | tf_op jit(solution)/shard_map/while/body/eval_jaxpr/stack | solution.py:99
  156.1 3.8 multiply_convert_fusion
  159.9 1.5 copy-done.2
  161.4 2.7 multiply_bitcast_fusion
  164.2 4.1 %stack.24 = f32[1,1,7,128,768]{3,2,4,1,0:T(8,128)} reshape(f32[896,12,64]{0,2,1:T(8,128)} %multiply_bitcast_fusion) | data formatting | bytes 5505024 | tf_op jit(solution)/shard_map/while/body/eval_jaxpr/stack | solution.py:99
  168.2 6.0 %maximum_bitcast_fusion = f32[7,2,128,768]{2,0,3,1:T(8,128)} fusion(f32[1,1,7,128,768]{3,2,4,1,0:T(8,128)} %stack.25, f32[1,1,7,128,768]{3,2,4,1,0:T(8,128)} %stack.24), kind=kLoop, calls=%fused_computation.3 | loop fusion | flops 1376256 | bytes 11010048 | tf_op jit(solution)/shard_map/while/body/eval_jaxpr/stack | solution.py:99
  174.3 6.4 %copy.44 = f32[7,2,128,768]{3,2,1,0:T(8,128)} copy(f32[7,2,128,768]{2,0,3,1:T(8,128)} %maximum_bitcast_fusion) | data formatting | bytes 11010048 | tf_op jit(solution)/shard_map/while/body/eval_jaxpr/stack | solution.py:99
  180.7 2.9 broadcast.96
  183.6 14.2 %scatter_fusion = f32[2,7,128,768]{3,2,1,0:T(8,128)} fusion(f32[2,7,128,768]{3,2,1,0:T(8,128)} %broadcast.96, s32[7]{0:T(128)S(1)} %fusion.23, f32[7,2,128,768]{3,2,1,0:T(8,128)} %copy.44), kind=kCustom, calls=%fused_computation.1 | custom fusion | flops 1376256 | bytes 16515100 | tf_op jit(solution)/shard_map/scatter-add | solution.py:114
  197.9 2.9 bitcast_convert_fusion
  200.8 1.1 fusion.26
  201.9 5.5 %collective-permute-start.11 = (bf16[2,1,1,128,768]{4,3,2,0,1:T(8,128)(2,1)S(1)}, bf16[2,1,1,128,768]{4,3,2,0,1:T(8,128)(2,1)S(1)}, u32[]{:S(2)}, u32[]{:S(2)}) collective-permute-start(bf16[2,1,1,128,768]{4,3,2,0,1:T(8,128)(2,1)S(1)} %get-tuple-element.48), channel_id=1, source_target_pairs={{0,3},{1,4},{2,5},{3,6},{4,7},{5,8},{6,9},{7,10},{8,11},{9,12},{10... | collective-permute-start | bytes 1179656 | tf_op jit(solution)/shard_map/ppermute | solution.py:16
  207.4 5.8 %collective-permute-start.10 = (bf16[2,1,1,128,768]{4,3,2,0,1:T(8,128)(2,1)}, bf16[2,1,1,128,768]{4,3,2,0,1:T(8,128)(2,1)S(1)}, u32[]{:S(2)}, u32[]{:S(2)}) collective-permute-start(bf16[2,1,1,128,768]{4,3,2,0,1:T(8,128)(2,1)} %get-tuple-element.49), channel_id=1, source_target_pairs={{0,2},{1,3},{2,4},{3,5},{4,6},{5,7},{6,8},{7,9},{8,10},{9,11},{10,... | collective-permute-start | bytes 1179656 | tf_op jit(solution)/shard_map/ppermute | solution.py:16
  213.2 3.4 collective-permute-start.9
  216.6 5.8 %collective-permute-start.8 = (bf16[2,1,1,128,768]{4,3,2,0,1:T(8,128)(2,1)}, bf16[2,1,1,128,768]{4,3,2,0,1:T(8,128)(2,1)}, u32[]{:S(2)}, u32[]{:S(2)}) collective-permute-start(bf16[2,1,1,128,768]{4,3,2,0,1:T(8,128)(2,1)} %get-tuple-element.51), channel_id=1, source_target_pairs={{0,63},{1,0},{2,1},{3,2},{4,3},{5,4},{6,5},{7,6},{8,7},{9,8},{10,9... | collective-permute-start | bytes 1179656 | tf_op jit(solution)/shard_map/ppermute | solution.py:16
  222.4 1.9 collective-permute-start.7
  224.3 17.2 %collective-permute-done.11 = bf16[2,1,1,128,768]{4,3,2,0,1:T(8,128)(2,1)S(1)} collective-permute-done((bf16[2,1,1,128,768]{4,3,2,0,1:T(8,128)(2,1)S(1)}, bf16[2,1,1,128,768]{4,3,2,0,1:T(8,128)(2,1)S(1)}, u32[]{:S(2)}, u32[]{:S(2)}) %collective-permute-start.11) | collective-permute-done | bytes 393248 | tf_op jit(solution)/shard_map/ppermute | solution.py:16
  241.6 4.7 %collective-permute-start.6 = (bf16[2,1,1,128,768]{4,3,2,0,1:T(8,128)(2,1)S(1)}, bf16[2,1,1,128,768]{4,3,2,0,1:T(8,128)(2,1)}, u32[]{:S(2)}, u32[]{:S(2)}) collective-permute-start(bf16[2,1,1,128,768]{4,3,2,0,1:T(8,128)(2,1)S(1)} %get-tuple-element.47), channel_id=1, source_target_pairs={{0,61},{1,62},{2,63},{3,0},{4,1},{5,2},{6,3},{7,4},{8,5},{9,6},{10... | collective-permute-start | bytes 1179656 | tf_op jit(solution)/shard_map/ppermute | solution.py:16
  247.0 0.8 copy.45
  247.8 1.0 fusion.10
  248.8 6.9 %collective-permute-done.10 = bf16[2,1,1,128,768]{4,3,2,0,1:T(8,128)(2,1)S(1)} collective-permute-done((bf16[2,1,1,128,768]{4,3,2,0,1:T(8,128)(2,1)}, bf16[2,1,1,128,768]{4,3,2,0,1:T(8,128)(2,1)S(1)}, u32[]{:S(2)}, u32[]{:S(2)}) %collective-permute-start.10) | collective-permute-done | bytes 393248 | tf_op jit(solution)/shard_map/ppermute | solution.py:16
  255.7 20.2 %collective-permute-done.9 = bf16[2,1,1,128,768]{4,3,2,0,1:T(8,128)(2,1)S(1)} collective-permute-done((bf16[2,1,1,128,768]{4,3,2,0,1:T(8,128)(2,1)}, bf16[2,1,1,128,768]{4,3,2,0,1:T(8,128)(2,1)S(1)}, u32[]{:S(2)}, u32[]{:S(2)}) %collective-permute-start.9) | collective-permute-done | bytes 393248 | tf_op jit(solution)/shard_map/ppermute | solution.py:16
  275.9 10.6 %collective-permute-done.6 = bf16[2,1,1,128,768]{4,3,2,0,1:T(8,128)(2,1)} collective-permute-done((bf16[2,1,1,128,768]{4,3,2,0,1:T(8,128)(2,1)S(1)}, bf16[2,1,1,128,768]{4,3,2,0,1:T(8,128)(2,1)}, u32[]{:S(2)}, u32[]{:S(2)}) %collective-permute-start.6) | collective-permute-done | bytes 393248 | tf_op jit(solution)/shard_map/ppermute | solution.py:16
  286.5 1.8 fusion.16
  288.3 0.8 slice_bitcast_fusion
  289.1 86.3 %all-gather.3.cloned.1.call-done = f32[6144,768]{1,0:T(8,128)} async-done(((f32[96,768]{1,0:T(8,128)}), f32[6144,768]{1,0:T(8,128)}) %all-gather.3.cloned.1.call-update) | async-done | bytes 18874384 | tf_op jit(solution)/shard_map/all_gather | solution.py:135
  375.4 7.3 %reduce_sum.31 = f32[96,768]{1,0:T(8,128)S(1)} reduce(f32[64,96,768]{2,1,0:T(8,128)} %bitcast.82, f32[]{:T(128)} %constant.88.clone.1), dimensions={0}, to_apply=%region_5.6 | reduce | flops 4644864 | bytes 19169284 | tf_op jit(solution)/shard_map/reduce_sum | solution.py:135
  382.8 0.7 broadcast_multiply_fusion
  (35 shorter events, 2.2 us)
Async XLA Ops:
  7.2 27.5 %copy-start = (bf16[768,768]{1,0:T(8,128)(2,1)S(1)}, bf16[768,768]{1,0:T(8,128)(2,1)}, u32[]{:S(2)}) copy-start(bf16[768,768]{1,0:T(8,128)(2,1)} %param.11) | copy-start | bytes 3538948
  7.2 30.0 %copy-start.9 = (bf16[1,1,128,768]{3,2,1,0:T(8,128)(2,1)S(1)}, bf16[1,1,128,768]{3,2,1,0:T(8,128)(2,1)}, u32[]{:S(2)}) copy-start(bf16[1,1,128,768]{3,2,1,0:T(8,128)(2,1)} %param.7) | copy-start | bytes 589828
  7.2 138.5 %reduce-scatter.2.cloned.1.call-start = ((), (), s32[]{:S(2)}) async-start(), calls=%async_computation.1 | async-start | bytes 1327104 | tf_op jit(solution)/shard_map/reduce_scatter | solution.py:127
  7.2 68.0 %copy-start.7 = (bf16[1,1,128,768]{3,2,1,0:T(8,128)(2,1)S(1)}, bf16[1,1,128,768]{3,2,1,0:T(8,128)(2,1)}, u32[]{:S(2)}) copy-start(bf16[1,1,128,768]{3,2,1,0:T(8,128)(2,1)} %param.9) | copy-start | bytes 589828
  7.2 68.0 %copy-start.8 = (bf16[1,1,128,768]{3,2,1,0:T(8,128)(2,1)S(1)}, bf16[1,1,128,768]{3,2,1,0:T(8,128)(2,1)}, u32[]{:S(2)}) copy-start(bf16[1,1,128,768]{3,2,1,0:T(8,128)(2,1)} %param.8) | copy-start | bytes 589828
  8.4 40.0 %collective-permute-start = (bf16[2,1,1,128,768]{4,3,2,1,0:T(8,128)(2,1)S(1)}, bf16[2,1,1,128,768]{4,3,2,1,0:T(8,128)(2,1)}, u32[]{:S(2)}, u32[]{:S(2)}) collective-permute-start(bf16[2,1,1,128,768]{4,3,2,1,0:T(8,128)(2,1)S(1)} %pad_maximum_fusion), channel_id=1, source_target_pairs={{0,3},{1,4},{2,5},{3,6},{4,7},{5,8},{6,9},{7,10},{8,11},{9,12},{10... | collective-permute-start | bytes 1179656 | tf_op jit(solution)/shard_map/ppermute | solution.py:16
  15.0 48.7 %collective-permute-start.1 = (bf16[2,1,1,128,768]{4,3,2,1,0:T(8,128)(2,1)S(1)}, bf16[2,1,1,128,768]{4,3,2,1,0:T(8,128)(2,1)}, u32[]{:S(2)}, u32[]{:S(2)}) collective-permute-start(bf16[2,1,1,128,768]{4,3,2,1,0:T(8,128)(2,1)S(1)} %pad_maximum_fusion), channel_id=1, source_target_pairs={{0,2},{1,3},{2,4},{3,5},{4,6},{5,7},{6,8},{7,9},{8,10},{9,11},{10,... | collective-permute-start | bytes 1179656 | tf_op jit(solution)/shard_map/ppermute | solution.py:16
  21.4 52.1 %collective-permute-start.2 = (bf16[2,1,1,128,768]{4,3,2,1,0:T(8,128)(2,1)S(1)}, bf16[2,1,1,128,768]{4,3,2,1,0:T(8,128)(2,1)}, u32[]{:S(2)}, u32[]{:S(2)}) collective-permute-start(bf16[2,1,1,128,768]{4,3,2,1,0:T(8,128)(2,1)S(1)} %pad_maximum_fusion), channel_id=1, source_target_pairs={{0,1},{1,2},{2,3},{3,4},{4,5},{5,6},{6,7},{7,8},{8,9},{9,10},{10,1... | collective-permute-start | bytes 1179656 | tf_op jit(solution)/shard_map/ppermute | solution.py:16
  25.2 50.8 %collective-permute-start.3 = (bf16[2,1,1,128,768]{4,3,2,1,0:T(8,128)(2,1)S(1)}, bf16[2,1,1,128,768]{4,3,2,1,0:T(8,128)(2,1)S(1)}, u32[]{:S(2)}, u32[]{:S(2)}) collective-permute-start(bf16[2,1,1,128,768]{4,3,2,1,0:T(8,128)(2,1)S(1)} %pad_maximum_fusion), channel_id=1, source_target_pairs={{0,63},{1,0},{2,1},{3,2},{4,3},{5,4},{6,5},{7,6},{8,7},{9,8},{10,9... | collective-permute-start | bytes 1179656 | tf_op jit(solution)/shard_map/ppermute | solution.py:16
  30.6 46.3 %collective-permute-start.4 = (bf16[2,1,1,128,768]{4,3,2,1,0:T(8,128)(2,1)S(1)}, bf16[2,1,1,128,768]{4,3,2,1,0:T(8,128)(2,1)S(1)}, u32[]{:S(2)}, u32[]{:S(2)}) collective-permute-start(bf16[2,1,1,128,768]{4,3,2,1,0:T(8,128)(2,1)S(1)} %pad_maximum_fusion), channel_id=1, source_target_pairs={{0,62},{1,63},{2,0},{3,1},{4,2},{5,3},{6,4},{7,5},{8,6},{9,7},{10,... | collective-permute-start | bytes 1179656 | tf_op jit(solution)/shard_map/ppermute | solution.py:16
  48.4 30.1 %collective-permute-start.5 = (bf16[2,1,1,128,768]{4,3,2,1,0:T(8,128)(2,1)S(1)}, bf16[2,1,1,128,768]{4,3,2,1,0:T(8,128)(2,1)S(1)}, u32[]{:S(2)}, u32[]{:S(2)}) collective-permute-start(bf16[2,1,1,128,768]{4,3,2,1,0:T(8,128)(2,1)S(1)} %pad_maximum_fusion), channel_id=1, source_target_pairs={{0,61},{1,62},{2,63},{3,0},{4,1},{5,2},{6,3},{7,4},{8,5},{9,6},{10... | collective-permute-start | bytes 1179656 | tf_op jit(solution)/shard_map/ppermute | solution.py:16
  102.4 4.8 %copy-start.5 = (bf16[896,12,64]{0,2,1:T(8,128)(2,1)S(1)}, bf16[896,12,64]{0,2,1:T(8,128)(2,1)}, u32[]{:S(2)}) copy-start(bf16[896,12,64]{0,2,1:T(8,128)(2,1)} %squeeze.36) | copy-start | bytes 4128772
  105.6 1.6 copy-start.1
  105.6 2.3 copy-start.6
  109.4 266.0 %all-gather.3.cloned.1.call-start = ((), (), s32[]{:S(2)}) async-start(), calls=%async_computation.2 | async-start | bytes 19169280 | tf_op jit(solution)/shard_map/all_gather | solution.py:135
  159.9 1.5 copy-start.2
  200.8 45.5 %copy-start.3 = (bf16[12,128,896]{1,2,0:T(8,128)(2,1)S(1)}, bf16[12,128,896]{1,2,0:T(8,128)(2,1)}, u32[]{:S(2)}) copy-start(bf16[12,128,896]{1,2,0:T(8,128)(2,1)} %copy-done.2) | copy-start | bytes 8257540
  200.8 45.5 %copy-start.4 = (bf16[896,12,64]{0,2,1:T(8,128)(2,1)S(1)}, bf16[896,12,64]{0,2,1:T(8,128)(2,1)}, u32[]{:S(2)}) copy-start(bf16[896,12,64]{0,2,1:T(8,128)(2,1)} %squeeze.37) | copy-start | bytes 4128772
  201.9 39.7 %collective-permute-start.11 = (bf16[2,1,1,128,768]{4,3,2,0,1:T(8,128)(2,1)S(1)}, bf16[2,1,1,128,768]{4,3,2,0,1:T(8,128)(2,1)S(1)}, u32[]{:S(2)}, u32[]{:S(2)}) collective-permute-start(bf16[2,1,1,128,768]{4,3,2,0,1:T(8,128)(2,1)S(1)} %get-tuple-element.48), channel_id=1, source_target_pairs={{0,3},{1,4},{2,5},{3,6},{4,7},{5,8},{6,9},{7,10},{8,11},{9,12},{10... | collective-permute-start | bytes 1179656 | tf_op jit(solution)/shard_map/ppermute | solution.py:16
  207.4 48.3 %collective-permute-start.10 = (bf16[2,1,1,128,768]{4,3,2,0,1:T(8,128)(2,1)}, bf16[2,1,1,128,768]{4,3,2,0,1:T(8,128)(2,1)S(1)}, u32[]{:S(2)}, u32[]{:S(2)}) collective-permute-start(bf16[2,1,1,128,768]{4,3,2,0,1:T(8,128)(2,1)} %get-tuple-element.49), channel_id=1, source_target_pairs={{0,2},{1,3},{2,4},{3,5},{4,6},{5,7},{6,8},{7,9},{8,10},{9,11},{10,... | collective-permute-start | bytes 1179656 | tf_op jit(solution)/shard_map/ppermute | solution.py:16
  213.2 62.7 %collective-permute-start.9 = (bf16[2,1,1,128,768]{4,3,2,0,1:T(8,128)(2,1)}, bf16[2,1,1,128,768]{4,3,2,0,1:T(8,128)(2,1)S(1)}, u32[]{:S(2)}, u32[]{:S(2)}) collective-permute-start(bf16[2,1,1,128,768]{4,3,2,0,1:T(8,128)(2,1)} %get-tuple-element.50), channel_id=1, source_target_pairs={{0,1},{1,2},{2,3},{3,4},{4,5},{5,6},{6,7},{7,8},{8,9},{9,10},{10,1... | collective-permute-start | bytes 1179656 | tf_op jit(solution)/shard_map/ppermute | solution.py:16
  216.6 59.3 %collective-permute-start.8 = (bf16[2,1,1,128,768]{4,3,2,0,1:T(8,128)(2,1)}, bf16[2,1,1,128,768]{4,3,2,0,1:T(8,128)(2,1)}, u32[]{:S(2)}, u32[]{:S(2)}) collective-permute-start(bf16[2,1,1,128,768]{4,3,2,0,1:T(8,128)(2,1)} %get-tuple-element.51), channel_id=1, source_target_pairs={{0,63},{1,0},{2,1},{3,2},{4,3},{5,4},{6,5},{7,6},{8,7},{9,8},{10,9... | collective-permute-start | bytes 1179656 | tf_op jit(solution)/shard_map/ppermute | solution.py:16
  222.4 53.5 %collective-permute-start.7 = (bf16[2,1,1,128,768]{4,3,2,0,1:T(8,128)(2,1)S(1)}, bf16[2,1,1,128,768]{4,3,2,0,1:T(8,128)(2,1)}, u32[]{:S(2)}, u32[]{:S(2)}) collective-permute-start(bf16[2,1,1,128,768]{4,3,2,0,1:T(8,128)(2,1)S(1)} %get-tuple-element.52), channel_id=1, source_target_pairs={{0,62},{1,63},{2,0},{3,1},{4,2},{5,3},{6,4},{7,5},{8,6},{9,7},{10,... | collective-permute-start | bytes 1179656 | tf_op jit(solution)/shard_map/ppermute | solution.py:16
  241.6 45.0 %collective-permute-start.6 = (bf16[2,1,1,128,768]{4,3,2,0,1:T(8,128)(2,1)S(1)}, bf16[2,1,1,128,768]{4,3,2,0,1:T(8,128)(2,1)}, u32[]{:S(2)}, u32[]{:S(2)}) collective-permute-start(bf16[2,1,1,128,768]{4,3,2,0,1:T(8,128)(2,1)S(1)} %get-tuple-element.47), channel_id=1, source_target_pairs={{0,61},{1,62},{2,63},{3,0},{4,1},{5,2},{6,3},{7,4},{8,5},{9,6},{10... | collective-permute-start | bytes 1179656 | tf_op jit(solution)/shard_map/ppermute | solution.py:16
Sparse Core Ops, SparseCore 0:
  109.5 36.0 reduce-scatter.1
  149.2 226.1 all-gather.2
